TPU v7x, 32 devices: a whole 2x2x4 slice. The times are simulated.
32 devices in a mesh: clip: 16 (over z, x, core), slab: 2 (over y).
Axes of the slice: x: 2, y: 2, z: 4, core: 2. Of those that a mesh axis runs over, the one named last changes fastest.
Arguments:
- frames_in: bfloat16 [32, 8, 128, 128], P('clip', 'slab')
- clip_ids: int32 [16], replicated, may hold values from 0 to 3, never falling along the last dimension, each value on 1 to 8 neighbouring positions
- gain_one: float32 [128], replicated, may hold values from 0.25 to 1.75
- shift_one: float32 [128], replicated, may hold values from -3 to 3
- kernel_one: bfloat16 [3, 3, 3, 128, 128], replicated, may hold values from -0.109375 to 0.109375
- bias_one: float32 [128], replicated, may hold values from -3 to 3
- gain_two: float32 [128], replicated, may hold values from 0.25 to 1.75
- shift_two: float32 [128], replicated, may hold values from -3 to 3
- kernel_two: bfloat16 [3, 3, 3, 128, 128], replicated, may hold values from -0.109375 to 0.109375
- bias_two: float32 [128], replicated, may hold values from -3 to 3
Outputs:
- frames_out: bfloat16 [32, 8, 128, 128], P('clip', 'slab')
Inputs may be any that keep to these rules, and one draw needn't show every extreme that they name: `clip_ids`: never falling along the blocks; each clip covers 1 to 8 blocks, one exactly 8.
All inputs are finite; a program needn't handle non-finite values.
Results may differ from a plain program's by a relative error of at most 0.0075.
Values may be sent and summed in bfloat16 or wider, within the bound.
No kernel may reach another device: no remote copies, remote signals or barrier semaphores. Data moves between devices by JAX's collectives and lax.ppermute only.
A program may use at most 64 MiB of HBM per device.

v0:
```python
import functools

import jax
import jax.numpy as jnp
from jax import lax
from jax.experimental import pallas as pl
from jax.experimental.pallas import tpu as pltpu
from jax.sharding import PartitionSpec as P


G = 32
BOTH = ("clip", "slab")
EPS = 1e-06


def moved(value, pairs):
    return lax.ppermute(value, BOTH, pairs)


def put_sums(first, second, sums_ref):
    both = jnp.concatenate([first, second], axis=0)
    sums_ref[...] = jnp.broadcast_to(both[None], sums_ref.shape)


def first_kernel(n_clip, n_slab, *refs):
    sources, refs = refs[:9], refs[9:]
    frames_ref, sums_ref, match_ref, table_ref, one_ref = refs[:5]
    edge_refs, (ids_ref, param_ref, sem) = refs[5:-3], refs[-3:]
    frames_hbm, ids_hbm, gain_one, shift_one, one_hbm, bias_one, gain_two, shift_two, bias_two = sources
    params = [gain_one, shift_one, bias_one, gain_two, shift_two, bias_two]
    copies = [
        pltpu.make_async_copy(frames_hbm, frames_ref, sem.at[0]),
        pltpu.make_async_copy(ids_hbm, ids_ref, sem.at[1]),
        pltpu.make_async_copy(one_hbm, one_ref, sem.at[2]),
    ]
    copies += [pltpu.make_async_copy(p, param_ref.at[i], sem.at[3 + i]) for i, p in enumerate(params)]
    for copy in copies:
        copy.start()
    frames, rows, cols, chans = frames_ref.shape
    slab = lax.axis_index("slab")
    position = lax.axis_index("clip")
    copies[0].wait()
    first = jnp.zeros((1, chans), jnp.float32)
    second = jnp.zeros((1, chans), jnp.float32)
    for f in range(frames):
        for r in range(rows):
            floats = frames_ref[f, r].astype(jnp.float32)
            first = first + jnp.sum(floats, axis=0, keepdims=True)
            second = second + jnp.sum(floats * floats, axis=0, keepdims=True)
    put_sums(first, second, sums_ref)
    if len(edge_refs) == 1:
        starts = [jnp.where(slab == 0, rows - 2, 0)]
    else:
        starts = [0, rows - 2]
    for edge_ref, start in zip(edge_refs, starts):
        for f in range(frames):
            for r in range(2):
                edge_ref[f, r] = frames_ref[f, start + r]
    copies[1].wait()
    own_clip = ids_ref[position]
    prior_clip = ids_ref[jnp.maximum(position - 1, 0)]
    same = jnp.logical_and(position > 0, prior_clip == own_clip).astype(jnp.float32)

    def add_block(b, blocks):
        weight = (ids_ref[b] == own_clip).astype(jnp.float32)
        for s in range(n_slab):
            match_ref[b * n_slab + s] = jnp.full((2, chans), weight, jnp.float32)
        return blocks + weight

    blocks = lax.fori_loop(0, n_clip, add_block, jnp.float32(0.0), unroll=n_clip <= 16)
    counts = blocks * float(frames * rows * n_slab * cols * (chans // G))
    for copy in copies[3:]:
        copy.wait()
    for i in range(len(params)):
        table_ref[i : i + 1] = param_ref[i : i + 1]
    table_ref[6:7] = jnp.full((1, chans), same, jnp.float32)
    table_ref[7:8] = jnp.full((1, chans), counts, jnp.float32)
    copies[2].wait()


def group_total(sums, per_group):
    lanes = lax.broadcasted_iota(jnp.int32, sums.shape, 1)
    width = 1
    while width < per_group:
        upper = pltpu.roll(sums, width, 1)
        lower = pltpu.roll(sums, sums.shape[1] - width, 1)
        sums = sums + jnp.where((lanes // width) % 2 == 0, lower, upper)
        width = 2 * width
    return sums


def half_affine(sums_ref, match_ref, table_ref, which):
    chans = table_ref.shape[1]
    total = jnp.sum(sums_ref[...] * match_ref[...], axis=0)
    moments = group_total(total, chans // G) / table_ref[7:8]
    mean, msq = moments[0:1], moments[1:2]
    scale = lax.rsqrt(msq - mean * mean + EPS) * table_ref[3 * which : 3 * which + 1]
    offset = table_ref[3 * which + 1 : 3 * which + 2] - mean * scale
    return 0.5 * scale, 0.5 * offset


def activate(raw, half_scale, half_offset):
    half = raw.astype(jnp.float32) * half_scale + half_offset
    return (half + half * jnp.tanh(half)).astype(jnp.bfloat16)


def products(act_ref, kernel_ref, frames, count, halves):
    cols, chans = act_ref.shape[2:]
    empty = jnp.zeros((chans, chans), jnp.bfloat16)

    def window(t):
        return [act_ref[t, dy : dy + count].reshape(count * cols, chans) for dy in range(3)]

    def weight(dt, dy, dx):
        return kernel_ref[dt, dy, dx] if 0 <= dt < 3 else empty

    def dot(windows, weights):
        return jnp.dot(
            jnp.concatenate(windows, axis=1), jnp.concatenate(weights, axis=0), preferred_element_type=jnp.float32
        )

    windows = [window(t) for t in range(frames + 2)]
    column = lax.broadcasted_iota(jnp.int32, (count * cols, chans), 0) % cols
    sides = [
        jnp.concatenate([weight(t - f, dy, 2) for f in range(frames)], axis=1)
        for t in range(frames + 2)
        for dy in range(3)
    ]
    pairs = [jnp.concatenate([weight(dt, dy, 0), weight(dt, dy, 1)], axis=1) for dt in range(3) for dy in range(3)]

    def finish(product, rights, f):
        left = pltpu.roll(product[:, :chans], 1, 0)
        right = pltpu.roll(rights[:, f * chans : (f + 1) * chans], count * cols - 1, 0)
        left = jnp.where(column == 0, 0.0, left)
        right = jnp.where(column == cols - 1, 0.0, right)
        return product[:, chans:] + left + right

    def main(f, part):
        return dot([w[part] for w in windows[f] + windows[f + 1] + windows[f + 2]], pairs)

    cut = (count + 1) // 2 * cols
    whole = slice(0, count * cols)
    if halves:
        mains = [jnp.concatenate([main(0, slice(0, cut)), main(0, slice(cut, count * cols))], axis=0)]
        rights = dot(sum(windows, []), sides)
        mains += [main(f, whole) for f in range(1, frames)]
    else:
        mains = [main(f, whole) for f in range(frames)]
        rights = dot(sum(windows, []), sides)
    for f in range(frames):
        yield f, finish(mains[f], rights, f)


def conv_one_kernel(n_slab, *refs):
    (two_hbm, sums_ref, match_ref, table_ref, kernel_ref, own_ref, prior_ref), refs = refs[:7], refs[7:]
    count = 1 if n_slab == 2 else 2
    beside, corner, refs = refs[:count], refs[count : 2 * count], refs[2 * count :]
    out_ref, next_sums_ref, two_ref, act_ref, sem = refs
    fetch = pltpu.make_async_copy(two_hbm, two_ref, sem.at[0])
    fetch.start()
    frames, rows, cols, chans = own_ref.shape
    out_rows = out_ref.shape[1]
    slab = lax.axis_index("slab")
    half_scale, half_offset = half_affine(sums_ref, match_ref, table_ref, 0)
    same = table_ref[6:7]
    empty = jnp.zeros((cols, chans), jnp.bfloat16)
    for at, body, borders, keep in ((0, prior_ref, corner, same), (frames, own_ref, beside, None)):
        scale = half_scale if keep is None else half_scale * keep
        offset = half_offset if keep is None else half_offset * keep
        for f in range(frames):
            if n_slab == 2:
                base = 1 + slab
                border = jnp.where(slab == 0, rows + 1, 0)
                act_ref[at + f, jnp.where(slab == 0, 0, rows + 2)] = empty
                for r in range(2):
                    act_ref[at + f, border + r] = activate(borders[0][f, r], scale, offset)
            else:
                base = 2
                has_up = (slab > 0).astype(jnp.float32)
                has_down = (slab < n_slab - 1).astype(jnp.float32)
                for r in range(2):
                    act_ref[at + f, r] = activate(borders[0][f, r], scale * has_up, offset * has_up)
                    act_ref[at + f, rows + 2 + r] = activate(borders[1][f, r], scale * has_down, offset * has_down)
            for r in range(rows):
                act_ref[at + f, base + r] = activate(body[f, r], scale, offset)
    first = jnp.zeros((1, chans), jnp.float32)
    second = jnp.zeros((1, chans), jnp.float32)
    own_base = slab if n_slab == 2 else 1
    for f, value in products(act_ref, kernel_ref, frames, out_rows, True):
        value = value + table_ref[2:3]
        value = value.reshape(out_rows, cols, chans)
        out_ref[f] = value.astype(jnp.bfloat16)
        for r in range(out_rows):
            inside = jnp.logical_and(r >= own_base, r < own_base + rows).astype(jnp.float32)
            floats = value[r]
            first = first + inside * jnp.sum(floats, axis=0, keepdims=True)
            second = second + inside * jnp.sum(floats * floats, axis=0, keepdims=True)
    put_sums(first, second, next_sums_ref)
    fetch.wait()


def conv_two_kernel(n_slab, sums_ref, match_ref, table_ref, kernel_ref, own_ref, prior_ref, residual_ref, out_hbm, act_ref, out_ref, sem):
    frames, rows, cols, chans = residual_ref.shape
    slab = lax.axis_index("slab")
    half_scale, half_offset = half_affine(sums_ref, match_ref, table_ref, 1)
    same = table_ref[6:7]
    empty = jnp.zeros((cols, chans), jnp.bfloat16)
    has_up = (slab > 0).astype(jnp.float32)
    has_down = (slab < n_slab - 1).astype(jnp.float32)
    count = own_ref.shape[1]
    stores = []
    for at, body, keep in ((0, prior_ref, same), (frames, own_ref, None)):
        scale = half_scale if keep is None else half_scale * keep
        offset = half_offset if keep is None else half_offset * keep
        for f in range(frames):
            if n_slab == 2:
                act_ref[at + f, jnp.where(slab == 0, 0, rows + 1)] = empty
                for r in range(count):
                    act_ref[at + f, 1 - slab + r] = activate(body[f, r], scale, offset)
            else:
                for r in range(count):
                    edge = has_up if r == 0 else has_down if r == count - 1 else 1.0
                    act_ref[at + f, r] = activate(body[f, r], scale * edge, offset * edge)
    for f, value in products(act_ref, kernel_ref, frames, rows, False):
        value = value + table_ref[5:6]
        value = value + residual_ref[f].reshape(rows * cols, chans).astype(jnp.float32)
        out_ref[f] = value.astype(jnp.bfloat16).reshape(rows, cols, chans)
        stores.append(pltpu.make_async_copy(out_ref.at[f], out_hbm.at[f], sem.at[f]))
        stores[-1].start()
    for store in stores:
        store.wait()


def per_device(n_clip, n_slab, *args):
    return block(n_clip, n_slab, *args)


def block(n_clip, n_slab, *args):
    frames_in, kernel = args[0], args[4]
    frames, rows, cols, chans = frames_in.shape
    count = 1 if n_slab == 2 else 2
    shape = jax.ShapeDtypeStruct
    sums_shape = shape((n_clip * n_slab, 2, chans), jnp.float32)
    vmem = pl.BlockSpec(memory_space=pltpu.VMEM)
    hbm = pl.BlockSpec(memory_space=pltpu.HBM)
    params = pltpu.CompilerParams(vmem_limit_bytes=24 << 20)

    def steps(dc, ds):
        return [
            (c * n_slab + s, (c + dc) * n_slab + s + ds)
            for c in range(n_clip - dc)
            for s in range(n_slab)
            if 0 <= s + ds < n_slab
        ]

    def call(kernel, outs, distant, operands, scratch, out_spec=vmem):
        distant = [pltpu.with_memory_space_constraint(x, pltpu.HBM) for x in distant]
        operands = distant + operands
        return pl.pallas_call(
            kernel,
            out_shape=outs,
            in_specs=[hbm] * len(distant) + [vmem] * (len(operands) - len(distant)),
            out_specs=jax.tree.map(lambda _: out_spec, outs),
            scratch_shapes=scratch,
            compiler_params=params,
        )(*operands)

    outs = [shape(frames_in.shape, frames_in.dtype), sums_shape, sums_shape, shape((8, chans), jnp.float32)]
    outs += [shape(kernel.shape, kernel.dtype)]
    outs += [shape((frames, 2, cols, chans), jnp.bfloat16)] * count
    scratch = [pltpu.SMEM((n_clip,), jnp.int32), pltpu.VMEM((6, chans), jnp.float32), pltpu.SemaphoreType.DMA((9,))]
    distant = [*args[:8], args[9]]
    frames_own, sums, match, table, kernel_one, *edges = call(
        functools.partial(first_kernel, n_clip, n_slab), outs, distant, [], scratch
    )
    if n_slab == 2:
        beside = [moved(edges[0], steps(0, 1) + steps(0, -1))]
        corner = [moved(edges[0], steps(1, 1) + steps(1, -1))]
    else:
        top, bottom = edges
        beside = [lax.ppermute(bottom, BOTH, steps(0, 1)), lax.ppermute(top, BOTH, steps(0, -1))]
        corner = [lax.ppermute(bottom, BOTH, steps(1, 1)), lax.ppermute(top, BOTH, steps(1, -1))]
    prior = moved(frames_own, steps(1, 0))
    sums = lax.all_to_all(sums, BOTH, 0, 0)
    hidden, sums, kernel_two = call(
        functools.partial(conv_one_kernel, n_slab),
        [shape((frames, rows + count, cols, chans), jnp.bfloat16), sums_shape, shape(kernel.shape, kernel.dtype)],
        [args[8]],
        [sums, match, table, kernel_one, frames_own, prior, *beside, *corner],
        [pltpu.VMEM((2 * frames, rows + 2 + count, cols, chans), jnp.bfloat16), pltpu.SemaphoreType.DMA((1,))],
    )
    prior = lax.ppermute(hidden, BOTH, steps(1, 0))
    sums = lax.all_to_all(sums, BOTH, 0, 0)
    return call(
        functools.partial(conv_two_kernel, n_slab),
        shape(frames_in.shape, jnp.bfloat16),
        [],
        [sums, match, table, kernel_two, hidden, prior, frames_own],
        [
            pltpu.VMEM((2 * frames, rows + 2, cols, chans), jnp.bfloat16),
            pltpu.VMEM(frames_in.shape, jnp.bfloat16),
            pltpu.SemaphoreType.DMA((frames,)),
        ],
        hbm,
    )


def solution(mesh):
    placed = (P("clip", "slab", None, None), P(), P(), P(), P(), P(), P(), P(), P(), P())
    return jax.shard_map(
        functools.partial(per_device, mesh.shape["clip"], mesh.shape["slab"]),
        mesh=mesh,
        in_specs=placed,
        out_specs=P("clip", "slab", None, None),
        check_vma=False,
    )
```

profile of v0, /device:TPU:0, one launch (start us, length us, event | category | flops | bytes accessed | tf_op | source)
XLA Modules:
  0.0 37.6 jit_solution(2805956217712234250)
XLA Ops:
  0.0 1.3 %shard_map.100 = (bf16[2,4,128,128]{3,2,1,0:T(8,128)(2,1)S(1)}, f32[32,2,128]{2,1,0:T(2,128)S(1)}, f32[32,2,128]{2,1,0:T(2,128)S(1)}, f32[8,128]{1,0:T(8,128)S(1...) custom-call(bf16[2,4,128,128]{3,2,1,0:T(8,128)(2,1)} %refs_0_.2, s32[16]{0:T(128)} %refs_1_.1, ...), custom_call_target="tpu_custom_call" | custom-call | tf_op jit(solution)/shard_map/pallas_call | solution.py:259
  1.3 2.4 %collective-permute-start = (bf16[2,4,128,128]{3,2,1,0:T(8,128)(2,1)S(1)}, bf16[2,4,128,128]{3,2,1,0:T(8,128)(2,1)S(1)}, u32[]{:S(2)}, u32[]{:S(2)}) collective-permute-start(bf16[2,4,128,128]{3,2,1,0:T(8,128)(2,1)S(1)} %get-tuple-element.18.refs_5_.residual_ref), channel_id=1, source_target_pairs={{0,2},{1,3},{2,4},{3,5},{4,6},{5,7},{6,8},{7,9},{8,10},{9,11},{10,... | collective-permute-start | bytes 786440 | tf_op jit(solution)/shard_map/ppermute | solution.py:17
  3.8 5.6 %collective-permute-start.2 = (bf16[2,2,128,128]{3,2,1,0:T(8,128)(2,1)S(1)}, bf16[2,2,128,128]{3,2,1,0:T(8,128)(2,1)S(1)}, u32[]{:S(2)}, u32[]{:S(2)}) collective-permute-start(bf16[2,2,128,128]{3,2,1,0:T(8,128)(2,1)S(1)} %get-tuple-element.19), channel_id=1, source_target_pairs={{0,3},{2,5},{4,7},{6,9},{8,11},{10,13},{12,15},{14,17},{16,19},{18... | collective-permute-start | bytes 393224 | tf_op jit(solution)/shard_map/ppermute | solution.py:17
  9.4 0.6 %collective-permute-start.1 = (bf16[2,2,128,128]{3,2,1,0:T(8,128)(2,1)S(1)}, bf16[2,2,128,128]{3,2,1,0:T(8,128)(2,1)S(1)}, u32[]{:S(2)}, u32[]{:S(2)}) collective-permute-start(bf16[2,2,128,128]{3,2,1,0:T(8,128)(2,1)S(1)} %get-tuple-element.19), channel_id=1, source_target_pairs={{0,1},{2,3},{4,5},{6,7},{8,9},{10,11},{12,13},{14,15},{16,17},{18,... | collective-permute-start | bytes 393224 | tf_op jit(solution)/shard_map/ppermute | solution.py:17
  10.0 12.1 %all_to_all.10.refs_1_ = f32[32,2,128]{2,1,0:T(2,128)S(1)} all-to-all(f32[32,2,128]{2,1,0:T(2,128)S(1)} %get-tuple-element.14), channel_id=1, replica_groups=mesh['clip'=16,'slab'=2] {'clip','slab'}, dimensions={0} | all-to-all | bytes 65536 | tf_op jit(solution)/shard_map/all_to_all | solution.py:284
  22.0 0.0 collective-permute-done.2.refs_8_
  22.0 0.0 collective-permute-done.1.refs_7_
  22.0 0.0 collective-permute-done.refs_6_
  22.0 2.0 %shard_map.101 = (bf16[2,5,128,128]{3,2,1,0:T(8,128)(2,1)S(1)}, f32[32,2,128]{2,1,0:T(2,128)S(1)}, bf16[3,3,3,128,128]{4,3,2,1,0:T(8,128)(2,1)S(1)}) custom-call(bf16[3,3,3,128,128]{4,3,2,1,0:T(8,128)(2,1)} %refs_0_.3, f32[32,2,128]{2,1,0:T(2,128)S(1)} %all_to_all.10.refs_1_, f32[32,2,128]{2,1,0:T(2,128)S(1)} %get-tuple-element.15.refs_2_.match_ref, ...), custom_call_target="tpu_custom_call" | custom-call | tf_op jit(solution)/shard_map/pallas_call | solution.py:259
  24.1 1.7 %collective-permute-start.3 = (bf16[2,5,128,128]{3,2,1,0:T(8,128)(2,1)S(1)}, bf16[2,5,128,128]{3,2,1,0:T(8,128)(2,1)S(1)}, u32[]{:S(2)}, u32[]{:S(2)}) collective-permute-start(bf16[2,5,128,128]{3,2,1,0:T(8,128)(2,1)S(1)} %get-tuple-element.22.own_ref), channel_id=1, source_target_pairs={{0,2},{1,3},{2,4},{3,5},{4,6},{5,7},{6,8},{7,9},{8,10},{9,11},{10,... | collective-permute-start | bytes 983048 | tf_op jit(solution)/shard_map/ppermute | solution.py:292
  25.8 9.5 %all_to_all.11.sums_ref = f32[32,2,128]{2,1,0:T(2,128)S(1)} all-to-all(f32[32,2,128]{2,1,0:T(2,128)S(1)} %get-tuple-element.20), channel_id=1, replica_groups=mesh['clip'=16,'slab'=2] {'clip','slab'}, dimensions={0} | all-to-all | bytes 65536 | tf_op jit(solution)/shard_map/all_to_all | solution.py:293
  35.3 0.0 collective-permute-done.3.prior_ref
  35.3 2.4 %shard_map.102 = bf16[2,4,128,128]{3,2,1,0:T(8,128)(2,1)} custom-call(f32[32,2,128]{2,1,0:T(2,128)S(1)} %all_to_all.11.sums_ref, f32[32,2,128]{2,1,0:T(2,128)S(1)} %get-tuple-element.15.refs_2_.match_ref, f32[8,128]{1,0:T(8,128)S(1)} %get-tuple-element.16.refs_3_.table_ref, bf16[3,3,3,128,128]{4,3,2,1,0:T(8,128)(2,1)S(1)} %get-tuple-element.21.kernel_ref, ...), custom_call_target="tpu_custom_call" | custom-call | tf_op jit(solution)/shard_map/pallas_call | solution.py:259
Async XLA Ops:
  1.3 20.7 %collective-permute-start = (bf16[2,4,128,128]{3,2,1,0:T(8,128)(2,1)S(1)}, bf16[2,4,128,128]{3,2,1,0:T(8,128)(2,1)S(1)}, u32[]{:S(2)}, u32[]{:S(2)}) collective-permute-start(bf16[2,4,128,128]{3,2,1,0:T(8,128)(2,1)S(1)} %get-tuple-element.18.refs_5_.residual_ref), channel_id=1, source_target_pairs={{0,2},{1,3},{2,4},{3,5},{4,6},{5,7},{6,8},{7,9},{8,10},{9,11},{10,... | collective-permute-start | bytes 786440 | tf_op jit(solution)/shard_map/ppermute | solution.py:17
  3.8 18.3 %collective-permute-start.2 = (bf16[2,2,128,128]{3,2,1,0:T(8,128)(2,1)S(1)}, bf16[2,2,128,128]{3,2,1,0:T(8,128)(2,1)S(1)}, u32[]{:S(2)}, u32[]{:S(2)}) collective-permute-start(bf16[2,2,128,128]{3,2,1,0:T(8,128)(2,1)S(1)} %get-tuple-element.19), channel_id=1, source_target_pairs={{0,3},{2,5},{4,7},{6,9},{8,11},{10,13},{12,15},{14,17},{16,19},{18... | collective-permute-start | bytes 393224 | tf_op jit(solution)/shard_map/ppermute | solution.py:17
  9.4 12.6 %collective-permute-start.1 = (bf16[2,2,128,128]{3,2,1,0:T(8,128)(2,1)S(1)}, bf16[2,2,128,128]{3,2,1,0:T(8,128)(2,1)S(1)}, u32[]{:S(2)}, u32[]{:S(2)}) collective-permute-start(bf16[2,2,128,128]{3,2,1,0:T(8,128)(2,1)S(1)} %get-tuple-element.19), channel_id=1, source_target_pairs={{0,1},{2,3},{4,5},{6,7},{8,9},{10,11},{12,13},{14,15},{16,17},{18,... | collective-permute-start | bytes 393224 | tf_op jit(solution)/shard_map/ppermute | solution.py:17
  24.1 11.2 %collective-permute-start.3 = (bf16[2,5,128,128]{3,2,1,0:T(8,128)(2,1)S(1)}, bf16[2,5,128,128]{3,2,1,0:T(8,128)(2,1)S(1)}, u32[]{:S(2)}, u32[]{:S(2)}) collective-permute-start(bf16[2,5,128,128]{3,2,1,0:T(8,128)(2,1)S(1)} %get-tuple-element.22.own_ref), channel_id=1, source_target_pairs={{0,2},{1,3},{2,4},{3,5},{4,6},{5,7},{6,8},{7,9},{8,10},{9,11},{10,... | collective-permute-start | bytes 983048 | tf_op jit(solution)/shard_map/ppermute | solution.py:292
where the time goes:
time: 37.9 us; the launch traced here: 37.6 us
  blocking collectives  21.5 us (57%)
  starting transfers between devices  10.3 us (27%)
  Pallas kernels  5.76 us (15%)
    all_to_all x2, blocking collectives, block(): sums = lax.all_to_all(sums, BOTH, 0, 0)  21.5 us
    ppermute x3, starting transfers between devices, moved(): return lax.ppermute(value, BOTH, pairs)  8.6 us
    pallas_call x3, Pallas kernels, call(): pl.pallas_call(kernel, out_shape=outs, in_specs=[hbm] * len(distant) + [v...  5.76 us
    ppermute x1, starting transfers between devices, block(): prior = lax.ppermute(hidden, BOTH, steps(1, 0))  1.68 us
  transfers between devices with their start and end apart: 4, of which 0 were waited for; matrix products, arithmetic and copies ran while one was open for 0% of the time, Pallas kernels for 0%

commit v1 on v0

--- a/solution.py
+++ b/solution.py
@@ -18,8 +18,10 @@
 
 
 def put_sums(first, second, sums_ref):
-    both = jnp.concatenate([first, second], axis=0)
-    sums_ref[...] = jnp.broadcast_to(both[None], sums_ref.shape)
+    totals = group_total(jnp.concatenate([first, second], axis=0), first.shape[1] // G)
+    even = lax.broadcasted_iota(jnp.int32, first.shape, 1) % 2 == 0
+    packed = jnp.where(even, totals[0:1], totals[1:2])
+    sums_ref[...] = jnp.broadcast_to(packed[None], sums_ref.shape)
 
 
 def first_kernel(n_clip, n_slab, *refs):
@@ -64,7 +66,7 @@
     def add_block(b, blocks):
         weight = (ids_ref[b] == own_clip).astype(jnp.float32)
         for s in range(n_slab):
-            match_ref[b * n_slab + s] = jnp.full((2, chans), weight, jnp.float32)
+            match_ref[b * n_slab + s] = jnp.full((1, chans), weight, jnp.float32)
         return blocks + weight
 
     blocks = lax.fori_loop(0, n_clip, add_block, jnp.float32(0.0), unroll=n_clip <= 16)
@@ -92,8 +94,9 @@
 def half_affine(sums_ref, match_ref, table_ref, which):
     chans = table_ref.shape[1]
     total = jnp.sum(sums_ref[...] * match_ref[...], axis=0)
-    moments = group_total(total, chans // G) / table_ref[7:8]
-    mean, msq = moments[0:1], moments[1:2]
+    even = lax.broadcasted_iota(jnp.int32, total.shape, 1) % 2 == 0
+    mean = jnp.where(even, total, pltpu.roll(total, 1, 1)) / table_ref[7:8]
+    msq = jnp.where(even, pltpu.roll(total, chans - 1, 1), total) / table_ref[7:8]
     scale = lax.rsqrt(msq - mean * mean + EPS) * table_ref[3 * which : 3 * which + 1]
     offset = table_ref[3 * which + 1 : 3 * which + 2] - mean * scale
     return 0.5 * scale, 0.5 * offset
@@ -240,7 +243,7 @@
     frames, rows, cols, chans = frames_in.shape
     count = 1 if n_slab == 2 else 2
     shape = jax.ShapeDtypeStruct
-    sums_shape = shape((n_clip * n_slab, 2, chans), jnp.float32)
+    sums_shape = shape((n_clip * n_slab, 1, chans), jnp.float32)
     vmem = pl.BlockSpec(memory_space=pltpu.VMEM)
     hbm = pl.BlockSpec(memory_space=pltpu.HBM)
     params = pltpu.CompilerParams(vmem_limit_bytes=24 << 20)

time: 37.9 us -> 37.6 us (level)
  no operation moved by 1% of the time
where the time goes in v1:
time: 37.6 us; the launch traced here: 37.4 us
  blocking collectives  21.3 us (57%)
  starting transfers between devices  10.3 us (27%)
  Pallas kernels  5.8 us (15%)
    all_to_all x2, blocking collectives, block(): sums = lax.all_to_all(sums, BOTH, 0, 0)  21.3 us
    ppermute x3, starting transfers between devices, moved(): return lax.ppermute(value, BOTH, pairs)  8.6 us
    pallas_call x3, Pallas kernels, call(): pl.pallas_call(kernel, out_shape=outs, in_specs=[hbm] * len(distant) + [v...  5.8 us
    ppermute x1, starting transfers between devices, block(): prior = lax.ppermute(hidden, BOTH, steps(1, 0))  1.71 us
  transfers between devices with their start and end apart: 4, of which 0 were waited for; matrix products, arithmetic and copies ran while one was open for 0% of the time, Pallas kernels for 0%

profile of v1, /device:TPU:0, one launch (start us, length us, event | category | flops | bytes accessed | tf_op | source)
XLA Modules:
  0.0 37.4 jit_solution(8347111909138136175)
XLA Ops:
  0.0 1.3 %shard_map.100 = (bf16[2,4,128,128]{3,2,1,0:T(8,128)(2,1)S(1)}, f32[32,1,128]{2,1,0:T(1,128)S(1)}, f32[32,1,128]{2,1,0:T(1,128)S(1)}, f32[8,128]{1,0:T(8,128)S(1...) custom-call(bf16[2,4,128,128]{3,2,1,0:T(8,128)(2,1)} %refs_0_.2, s32[16]{0:T(128)} %refs_1_.1, ...), custom_call_target="tpu_custom_call" | custom-call | tf_op jit(solution)/shard_map/pallas_call | solution.py:262
  1.3 2.4 %collective-permute-start = (bf16[2,4,128,128]{3,2,1,0:T(8,128)(2,1)S(1)}, bf16[2,4,128,128]{3,2,1,0:T(8,128)(2,1)S(1)}, u32[]{:S(2)}, u32[]{:S(2)}) collective-permute-start(bf16[2,4,128,128]{3,2,1,0:T(8,128)(2,1)S(1)} %get-tuple-element.18.refs_5_.residual_ref), channel_id=1, source_target_pairs={{0,2},{1,3},{2,4},{3,5},{4,6},{5,7},{6,8},{7,9},{8,10},{9,11},{10,... | collective-permute-start | bytes 786440 | tf_op jit(solution)/shard_map/ppermute | solution.py:17
  3.8 5.6 %collective-permute-start.2 = (bf16[2,2,128,128]{3,2,1,0:T(8,128)(2,1)S(1)}, bf16[2,2,128,128]{3,2,1,0:T(8,128)(2,1)S(1)}, u32[]{:S(2)}, u32[]{:S(2)}) collective-permute-start(bf16[2,2,128,128]{3,2,1,0:T(8,128)(2,1)S(1)} %get-tuple-element.19), channel_id=1, source_target_pairs={{0,3},{2,5},{4,7},{6,9},{8,11},{10,13},{12,15},{14,17},{16,19},{18... | collective-permute-start | bytes 393224 | tf_op jit(solution)/shard_map/ppermute | solution.py:17
  9.4 0.6 %collective-permute-start.1 = (bf16[2,2,128,128]{3,2,1,0:T(8,128)(2,1)S(1)}, bf16[2,2,128,128]{3,2,1,0:T(8,128)(2,1)S(1)}, u32[]{:S(2)}, u32[]{:S(2)}) collective-permute-start(bf16[2,2,128,128]{3,2,1,0:T(8,128)(2,1)S(1)} %get-tuple-element.19), channel_id=1, source_target_pairs={{0,1},{2,3},{4,5},{6,7},{8,9},{10,11},{12,13},{14,15},{16,17},{18,... | collective-permute-start | bytes 393224 | tf_op jit(solution)/shard_map/ppermute | solution.py:17
  10.0 11.9 %all_to_all.10.refs_1_ = f32[32,1,128]{2,1,0:T(1,128)S(1)} all-to-all(f32[32,1,128]{2,1,0:T(1,128)S(1)} %get-tuple-element.14), channel_id=1, replica_groups=mesh['clip'=16,'slab'=2] {'clip','slab'}, dimensions={0} | all-to-all | bytes 32768 | tf_op jit(solution)/shard_map/all_to_all | solution.py:287
  21.9 0.0 collective-permute-done.2.refs_8_
  21.9 0.0 collective-permute-done.1.refs_7_
  21.9 0.0 collective-permute-done.refs_6_
  21.9 2.2 %shard_map.101 = (bf16[2,5,128,128]{3,2,1,0:T(8,128)(2,1)S(1)}, f32[32,1,128]{2,1,0:T(1,128)S(1)}, bf16[3,3,3,128,128]{4,3,2,1,0:T(8,128)(2,1)S(1)}) custom-call(bf16[3,3,3,128,128]{4,3,2,1,0:T(8,128)(2,1)} %refs_0_.3, f32[32,1,128]{2,1,0:T(1,128)S(1)} %all_to_all.10.refs_1_, f32[32,1,128]{2,1,0:T(1,128)S(1)} %get-tuple-element.15.refs_2_.match_ref, ...), custom_call_target="tpu_custom_call" | custom-call | tf_op jit(solution)/shard_map/pallas_call | solution.py:262
  24.1 1.7 %collective-permute-start.3 = (bf16[2,5,128,128]{3,2,1,0:T(8,128)(2,1)S(1)}, bf16[2,5,128,128]{3,2,1,0:T(8,128)(2,1)S(1)}, u32[]{:S(2)}, u32[]{:S(2)}) collective-permute-start(bf16[2,5,128,128]{3,2,1,0:T(8,128)(2,1)S(1)} %get-tuple-element.22.own_ref), channel_id=1, source_target_pairs={{0,2},{1,3},{2,4},{3,5},{4,6},{5,7},{6,8},{7,9},{8,10},{9,11},{10,... | collective-permute-start | bytes 983048 | tf_op jit(solution)/shard_map/ppermute | solution.py:295
  25.8 9.3 %all_to_all.11.sums_ref = f32[32,1,128]{2,1,0:T(1,128)S(1)} all-to-all(f32[32,1,128]{2,1,0:T(1,128)S(1)} %get-tuple-element.20), channel_id=1, replica_groups=mesh['clip'=16,'slab'=2] {'clip','slab'}, dimensions={0} | all-to-all | bytes 32768 | tf_op jit(solution)/shard_map/all_to_all | solution.py:296
  35.1 0.0 collective-permute-done.3.prior_ref
  35.1 2.3 %shard_map.102 = bf16[2,4,128,128]{3,2,1,0:T(8,128)(2,1)} custom-call(f32[32,1,128]{2,1,0:T(1,128)S(1)} %all_to_all.11.sums_ref, f32[32,1,128]{2,1,0:T(1,128)S(1)} %get-tuple-element.15.refs_2_.match_ref, f32[8,128]{1,0:T(8,128)S(1)} %get-tuple-element.16.refs_3_.table_ref, bf16[3,3,3,128,128]{4,3,2,1,0:T(8,128)(2,1)S(1)} %get-tuple-element.21.kernel_ref, ...), custom_call_target="tpu_custom_call" | custom-call | tf_op jit(solution)/shard_map/pallas_call | solution.py:262
Async XLA Ops:
  1.3 20.6 %collective-permute-start = (bf16[2,4,128,128]{3,2,1,0:T(8,128)(2,1)S(1)}, bf16[2,4,128,128]{3,2,1,0:T(8,128)(2,1)S(1)}, u32[]{:S(2)}, u32[]{:S(2)}) collective-permute-start(bf16[2,4,128,128]{3,2,1,0:T(8,128)(2,1)S(1)} %get-tuple-element.18.refs_5_.residual_ref), channel_id=1, source_target_pairs={{0,2},{1,3},{2,4},{3,5},{4,6},{5,7},{6,8},{7,9},{8,10},{9,11},{10,... | collective-permute-start | bytes 786440 | tf_op jit(solution)/shard_map/ppermute | solution.py:17
  3.8 18.1 %collective-permute-start.2 = (bf16[2,2,128,128]{3,2,1,0:T(8,128)(2,1)S(1)}, bf16[2,2,128,128]{3,2,1,0:T(8,128)(2,1)S(1)}, u32[]{:S(2)}, u32[]{:S(2)}) collective-permute-start(bf16[2,2,128,128]{3,2,1,0:T(8,128)(2,1)S(1)} %get-tuple-element.19), channel_id=1, source_target_pairs={{0,3},{2,5},{4,7},{6,9},{8,11},{10,13},{12,15},{14,17},{16,19},{18... | collective-permute-start | bytes 393224 | tf_op jit(solution)/shard_map/ppermute | solution.py:17
  9.4 12.5 %collective-permute-start.1 = (bf16[2,2,128,128]{3,2,1,0:T(8,128)(2,1)S(1)}, bf16[2,2,128,128]{3,2,1,0:T(8,128)(2,1)S(1)}, u32[]{:S(2)}, u32[]{:S(2)}) collective-permute-start(bf16[2,2,128,128]{3,2,1,0:T(8,128)(2,1)S(1)} %get-tuple-element.19), channel_id=1, source_target_pairs={{0,1},{2,3},{4,5},{6,7},{8,9},{10,11},{12,13},{14,15},{16,17},{18,... | collective-permute-start | bytes 393224 | tf_op jit(solution)/shard_map/ppermute | solution.py:17
  24.1 11.0 %collective-permute-start.3 = (bf16[2,5,128,128]{3,2,1,0:T(8,128)(2,1)S(1)}, bf16[2,5,128,128]{3,2,1,0:T(8,128)(2,1)S(1)}, u32[]{:S(2)}, u32[]{:S(2)}) collective-permute-start(bf16[2,5,128,128]{3,2,1,0:T(8,128)(2,1)S(1)} %get-tuple-element.22.own_ref), channel_id=1, source_target_pairs={{0,2},{1,3},{2,4},{3,5},{4,6},{5,7},{6,8},{7,9},{8,10},{9,11},{10,... | collective-permute-start | bytes 983048 | tf_op jit(solution)/shard_map/ppermute | solution.py:295

commit v2 on v1

--- a/solution.py
+++ b/solution.py
@@ -160,7 +160,6 @@
     beside, corner, refs = refs[:count], refs[count : 2 * count], refs[2 * count :]
     out_ref, next_sums_ref, two_ref, act_ref, sem = refs
     fetch = pltpu.make_async_copy(two_hbm, two_ref, sem.at[0])
-    fetch.start()
     frames, rows, cols, chans = own_ref.shape
     out_rows = out_ref.shape[1]
     slab = lax.axis_index("slab")
@@ -186,6 +185,7 @@
                     act_ref[at + f, rows + 2 + r] = activate(borders[1][f, r], scale * has_down, offset * has_down)
             for r in range(rows):
                 act_ref[at + f, base + r] = activate(body[f, r], scale, offset)
+    fetch.start()
     first = jnp.zeros((1, chans), jnp.float32)
     second = jnp.zeros((1, chans), jnp.float32)
     own_base = slab if n_slab == 2 else 1
@@ -227,9 +227,12 @@
     for f, value in products(act_ref, kernel_ref, frames, rows, False):
         value = value + table_ref[5:6]
         value = value + residual_ref[f].reshape(rows * cols, chans).astype(jnp.float32)
-        out_ref[f] = value.astype(jnp.bfloat16).reshape(rows, cols, chans)
-        stores.append(pltpu.make_async_copy(out_ref.at[f], out_hbm.at[f], sem.at[f]))
-        stores[-1].start()
+        value = value.astype(jnp.bfloat16).reshape(rows, cols, chans)
+        for part in range(2):
+            piece = pl.ds(part * (rows // 2), rows // 2)
+            out_ref[f, piece] = value[part * (rows // 2) : (part + 1) * (rows // 2)]
+            stores.append(pltpu.make_async_copy(out_ref.at[f, piece], out_hbm.at[f, piece], sem.at[2 * f + part]))
+            stores[-1].start()
     for store in stores:
         store.wait()
 
@@ -302,7 +305,7 @@
         [
             pltpu.VMEM((2 * frames, rows + 2, cols, chans), jnp.bfloat16),
             pltpu.VMEM(frames_in.shape, jnp.bfloat16),
-            pltpu.SemaphoreType.DMA((frames,)),
+            pltpu.SemaphoreType.DMA((2 * frames,)),
         ],
         hbm,
     )

time: 37.6 us -> 37.6 us (level)
  no operation moved by 1% of the time
where the time goes in v2:
time: 37.6 us; the launch traced here: 37.4 us
  blocking collectives  21.3 us (57%)
  starting transfers between devices  10.3 us (27%)
  Pallas kernels  5.79 us (15%)
    all_to_all x2, blocking collectives, block(): sums = lax.all_to_all(sums, BOTH, 0, 0)  21.3 us
    ppermute x3, starting transfers between devices, moved(): return lax.ppermute(value, BOTH, pairs)  8.6 us
    pallas_call x3, Pallas kernels, call(): pl.pallas_call(kernel, out_shape=outs, in_specs=[hbm] * len(distant) + [v...  5.79 us
    ppermute x1, starting transfers between devices, block(): prior = lax.ppermute(hidden, BOTH, steps(1, 0))  1.71 us
  transfers between devices with their start and end apart: 4, of which 0 were waited for; matrix products, arithmetic and copies ran while one was open for 0% of the time, Pallas kernels for 0%

profile of v2, /device:TPU:0, one launch (start us, length us, event | category | flops | bytes accessed | tf_op | source)
XLA Modules:
  0.0 37.4 jit_solution(13819099404316707996)
XLA Ops:
  0.0 1.3 %shard_map.100 = (bf16[2,4,128,128]{3,2,1,0:T(8,128)(2,1)S(1)}, f32[32,1,128]{2,1,0:T(1,128)S(1)}, f32[32,1,128]{2,1,0:T(1,128)S(1)}, f32[8,128]{1,0:T(8,128)S(1...) custom-call(bf16[2,4,128,128]{3,2,1,0:T(8,128)(2,1)} %refs_0_.2, s32[16]{0:T(128)} %refs_1_.1, ...), custom_call_target="tpu_custom_call" | custom-call | tf_op jit(solution)/shard_map/pallas_call | solution.py:265
  1.3 2.4 %collective-permute-start = (bf16[2,4,128,128]{3,2,1,0:T(8,128)(2,1)S(1)}, bf16[2,4,128,128]{3,2,1,0:T(8,128)(2,1)S(1)}, u32[]{:S(2)}, u32[]{:S(2)}) collective-permute-start(bf16[2,4,128,128]{3,2,1,0:T(8,128)(2,1)S(1)} %get-tuple-element.18.refs_5_.residual_ref), channel_id=1, source_target_pairs={{0,2},{1,3},{2,4},{3,5},{4,6},{5,7},{6,8},{7,9},{8,10},{9,11},{10,... | collective-permute-start | bytes 786440 | tf_op jit(solution)/shard_map/ppermute | solution.py:17
  3.8 5.6 %collective-permute-start.2 = (bf16[2,2,128,128]{3,2,1,0:T(8,128)(2,1)S(1)}, bf16[2,2,128,128]{3,2,1,0:T(8,128)(2,1)S(1)}, u32[]{:S(2)}, u32[]{:S(2)}) collective-permute-start(bf16[2,2,128,128]{3,2,1,0:T(8,128)(2,1)S(1)} %get-tuple-element.19), channel_id=1, source_target_pairs={{0,3},{2,5},{4,7},{6,9},{8,11},{10,13},{12,15},{14,17},{16,19},{18... | collective-permute-start | bytes 393224 | tf_op jit(solution)/shard_map/ppermute | solution.py:17
  9.4 0.6 %collective-permute-start.1 = (bf16[2,2,128,128]{3,2,1,0:T(8,128)(2,1)S(1)}, bf16[2,2,128,128]{3,2,1,0:T(8,128)(2,1)S(1)}, u32[]{:S(2)}, u32[]{:S(2)}) collective-permute-start(bf16[2,2,128,128]{3,2,1,0:T(8,128)(2,1)S(1)} %get-tuple-element.19), channel_id=1, source_target_pairs={{0,1},{2,3},{4,5},{6,7},{8,9},{10,11},{12,13},{14,15},{16,17},{18,... | collective-permute-start | bytes 393224 | tf_op jit(solution)/shard_map/ppermute | solution.py:17
  10.0 11.9 %all_to_all.10.refs_1_ = f32[32,1,128]{2,1,0:T(1,128)S(1)} all-to-all(f32[32,1,128]{2,1,0:T(1,128)S(1)} %get-tuple-element.14), channel_id=1, replica_groups=mesh['clip'=16,'slab'=2] {'clip','slab'}, dimensions={0} | all-to-all | bytes 32768 | tf_op jit(solution)/shard_map/all_to_all | solution.py:290
  21.9 0.0 collective-permute-done.2.refs_8_
  21.9 0.0 collective-permute-done.1.refs_7_
  21.9 0.0 collective-permute-done.refs_6_
  21.9 2.2 %shard_map.101 = (bf16[2,5,128,128]{3,2,1,0:T(8,128)(2,1)S(1)}, f32[32,1,128]{2,1,0:T(1,128)S(1)}, bf16[3,3,3,128,128]{4,3,2,1,0:T(8,128)(2,1)S(1)}) custom-call(bf16[3,3,3,128,128]{4,3,2,1,0:T(8,128)(2,1)} %refs_0_.3, f32[32,1,128]{2,1,0:T(1,128)S(1)} %all_to_all.10.refs_1_, f32[32,1,128]{2,1,0:T(1,128)S(1)} %get-tuple-element.15.refs_2_.match_ref, ...), custom_call_target="tpu_custom_call" | custom-call | tf_op jit(solution)/shard_map/pallas_call | solution.py:265
  24.1 1.7 %collective-permute-start.3 = (bf16[2,5,128,128]{3,2,1,0:T(8,128)(2,1)S(1)}, bf16[2,5,128,128]{3,2,1,0:T(8,128)(2,1)S(1)}, u32[]{:S(2)}, u32[]{:S(2)}) collective-permute-start(bf16[2,5,128,128]{3,2,1,0:T(8,128)(2,1)S(1)} %get-tuple-element.22.own_ref), channel_id=1, source_target_pairs={{0,2},{1,3},{2,4},{3,5},{4,6},{5,7},{6,8},{7,9},{8,10},{9,11},{10,... | collective-permute-start | bytes 983048 | tf_op jit(solution)/shard_map/ppermute | solution.py:298
  25.8 9.3 %all_to_all.11.sums_ref = f32[32,1,128]{2,1,0:T(1,128)S(1)} all-to-all(f32[32,1,128]{2,1,0:T(1,128)S(1)} %get-tuple-element.20), channel_id=1, replica_groups=mesh['clip'=16,'slab'=2] {'clip','slab'}, dimensions={0} | all-to-all | bytes 32768 | tf_op jit(solution)/shard_map/all_to_all | solution.py:299
  35.1 0.0 collective-permute-done.3.prior_ref
  35.1 2.3 %shard_map.102 = bf16[2,4,128,128]{3,2,1,0:T(8,128)(2,1)} custom-call(f32[32,1,128]{2,1,0:T(1,128)S(1)} %all_to_all.11.sums_ref, f32[32,1,128]{2,1,0:T(1,128)S(1)} %get-tuple-element.15.refs_2_.match_ref, f32[8,128]{1,0:T(8,128)S(1)} %get-tuple-element.16.refs_3_.table_ref, bf16[3,3,3,128,128]{4,3,2,1,0:T(8,128)(2,1)S(1)} %get-tuple-element.21.kernel_ref, ...), custom_call_target="tpu_custom_call" | custom-call | tf_op jit(solution)/shard_map/pallas_call | solution.py:265
Async XLA Ops:
  1.3 20.6 %collective-permute-start = (bf16[2,4,128,128]{3,2,1,0:T(8,128)(2,1)S(1)}, bf16[2,4,128,128]{3,2,1,0:T(8,128)(2,1)S(1)}, u32[]{:S(2)}, u32[]{:S(2)}) collective-permute-start(bf16[2,4,128,128]{3,2,1,0:T(8,128)(2,1)S(1)} %get-tuple-element.18.refs_5_.residual_ref), channel_id=1, source_target_pairs={{0,2},{1,3},{2,4},{3,5},{4,6},{5,7},{6,8},{7,9},{8,10},{9,11},{10,... | collective-permute-start | bytes 786440 | tf_op jit(solution)/shard_map/ppermute | solution.py:17
  3.8 18.1 %collective-permute-start.2 = (bf16[2,2,128,128]{3,2,1,0:T(8,128)(2,1)S(1)}, bf16[2,2,128,128]{3,2,1,0:T(8,128)(2,1)S(1)}, u32[]{:S(2)}, u32[]{:S(2)}) collective-permute-start(bf16[2,2,128,128]{3,2,1,0:T(8,128)(2,1)S(1)} %get-tuple-element.19), channel_id=1, source_target_pairs={{0,3},{2,5},{4,7},{6,9},{8,11},{10,13},{12,15},{14,17},{16,19},{18... | collective-permute-start | bytes 393224 | tf_op jit(solution)/shard_map/ppermute | solution.py:17
  9.4 12.5 %collective-permute-start.1 = (bf16[2,2,128,128]{3,2,1,0:T(8,128)(2,1)S(1)}, bf16[2,2,128,128]{3,2,1,0:T(8,128)(2,1)S(1)}, u32[]{:S(2)}, u32[]{:S(2)}) collective-permute-start(bf16[2,2,128,128]{3,2,1,0:T(8,128)(2,1)S(1)} %get-tuple-element.19), channel_id=1, source_target_pairs={{0,1},{2,3},{4,5},{6,7},{8,9},{10,11},{12,13},{14,15},{16,17},{18,... | collective-permute-start | bytes 393224 | tf_op jit(solution)/shard_map/ppermute | solution.py:17
  24.1 11.0 %collective-permute-start.3 = (bf16[2,5,128,128]{3,2,1,0:T(8,128)(2,1)S(1)}, bf16[2,5,128,128]{3,2,1,0:T(8,128)(2,1)S(1)}, u32[]{:S(2)}, u32[]{:S(2)}) collective-permute-start(bf16[2,5,128,128]{3,2,1,0:T(8,128)(2,1)S(1)} %get-tuple-element.22.own_ref), channel_id=1, source_target_pairs={{0,2},{1,3},{2,4},{3,5},{4,6},{5,7},{6,8},{7,9},{8,10},{9,11},{10,... | collective-permute-start | bytes 983048 | tf_op jit(solution)/shard_map/ppermute | solution.py:298
